TPU v7x, 32 devices: a whole 2x2x4 slice. The times are simulated.
32 devices in a mesh: blk: 8 (over z, x), uly: 4 (over y, core).
Axes of the slice: x: 2, y: 2, z: 4, core: 2. Of those that a mesh axis runs over, the one named last changes fastest.
Arguments:
- query_projection: bfloat16 [4096, 4096], P(('blk', 'uly')), may hold values from -4.5 to 4.5
- key_projection: bfloat16 [4096, 512], P(('blk', 'uly')), may hold values from -4.5 to 4.5
- value_projection: bfloat16 [4096, 512], P(('blk', 'uly')), may hold values from -6 to 6
- doc_start: int32 [4096], P('blk'), may hold values from 0 to 4095, as said below
Outputs:
- attn: bfloat16 [4096, 4096], P(('blk', 'uly'))
Inputs may be any that keep to these rules, and one draw needn't show every extreme that they name: Documents are contiguous runs of positions: doc_start[0] = 0, doc_start never falls, doc_start[i] <= i, and doc_start[doc_start[i]] = doc_start[i]. Every document has at most 1024 positions; the first has exactly 1024, and another of exactly 1024 begins strictly inside a block of 512 positions. The last position begins a document of its own.
All inputs are finite; a program needn't handle non-finite values.
Results may differ from a plain program's by a relative error of at most 0.0031.
Values may be sent and summed in bfloat16 or wider, within the bound.
A program may use at most 64 MiB of HBM per device.

v0:
```python
import jax
import jax.numpy as jnp
from jax import lax
from jax.sharding import PartitionSpec as P

HEAD_WIDTH = 128
CYCLE_STEPS = 2
POSITION_GROUP = 512


masked_score = -1e30


def from_behind(block, axis, distance):
    devices = range(lax.axis_size(axis))
    route = [(i - distance, i) for i in devices if i - distance in devices]
    return lax.ppermute(block, axis, route)


def local(query_projection, key_projection, value_projection, doc_start):
    width = lax.axis_size("uly")
    tokens_dev = query_projection.shape[0]
    kv_heads = key_projection.shape[1] // HEAD_WIDTH
    repeats = max(1, width // kv_heads)

    def widen_heads(source):
        split_heads = source.reshape(tokens_dev, kv_heads, 1, HEAD_WIDTH)
        copies = jnp.broadcast_to(split_heads, (tokens_dev, kv_heads, repeats, HEAD_WIDTH))
        return copies.reshape(tokens_dev, kv_heads * repeats * HEAD_WIDTH)

    query_rows = lax.all_to_all(query_projection, "uly", split_axis=1, concat_axis=0, tiled=True)
    key_rows, value_rows = (
        lax.all_to_all(widen_heads(key_projection), "uly", split_axis=1, concat_axis=0, tiled=True),
        lax.all_to_all(
            widen_heads(value_projection), "uly", split_axis=1, concat_axis=0, tiled=True
        ),
    )
    row_count = query_rows.shape[0]
    local_kv = key_rows.shape[1] // HEAD_WIDTH
    local_q = query_rows.shape[1] // HEAD_WIDTH
    query_group_width = local_q // local_kv
    earlier = []
    for step in range(CYCLE_STEPS):
        earlier.insert(0, from_behind((key_rows, value_rows), "blk", step + 1))
    joined_keys = jnp.concatenate([piece[0] for piece in earlier] + [key_rows], axis=0).reshape(
        -1, local_kv, HEAD_WIDTH
    )
    joined_values = jnp.concatenate([piece[1] for piece in earlier] + [value_rows], axis=0).reshape(
        -1, local_kv, HEAD_WIDTH
    )
    lead = CYCLE_STEPS * row_count
    base = lax.axis_index("blk") * row_count
    anchor = base - lead
    query_heads = query_rows.reshape(row_count, local_kv, query_group_width, HEAD_WIDTH)
    score_scale = HEAD_WIDTH ** (-0.5)

    def one_tile(index):
        start = index * POSITION_GROUP
        query_tile = lax.dynamic_slice_in_dim(query_heads, start, POSITION_GROUP, 0)
        starts = lax.dynamic_slice_in_dim(doc_start, start, POSITION_GROUP, 0)
        query_places = base + start + jnp.arange(POSITION_GROUP, dtype=jnp.int32)
        first_tile = (jnp.min(starts) - anchor) // POSITION_GROUP
        last_tile = (lead + start) // POSITION_GROUP

        def add_tile(tile, carry):
            running_maximum, running_sum, running_output = carry
            key_start = tile * POSITION_GROUP
            key_tile = lax.dynamic_slice_in_dim(joined_keys, key_start, POSITION_GROUP, 0)
            value_tile = lax.dynamic_slice_in_dim(joined_values, key_start, POSITION_GROUP, 0)
            key_places = anchor + key_start + jnp.arange(POSITION_GROUP, dtype=jnp.int32)
            seen = (key_places[None, :] >= starts[:, None]) & (
                key_places[None, :] <= query_places[:, None]
            )
            seen = seen[:, None, None, :]
            scores = (
                jnp.einsum(
                    "tkgd,nkd->tkgn", query_tile, key_tile, preferred_element_type=jnp.float32
                )
                * score_scale
            )
            masked = jnp.where(seen, scores, masked_score)
            fresh = jnp.maximum(running_maximum, jnp.max(masked, axis=-1))
            factor = jnp.exp(running_maximum - fresh)
            exps = jnp.where(seen, jnp.exp(masked - fresh[..., None]), 0.0)
            running_sum = running_sum * factor + jnp.sum(exps, axis=-1)
            blended = jnp.einsum(
                "tkgn,nkd->tkgd",
                exps.astype(jnp.bfloat16),
                value_tile,
                preferred_element_type=jnp.float32,
            )
            running_output = running_output * factor[..., None] + blended
            return (fresh, running_sum, running_output)

        running_maximum = jnp.full(
            (POSITION_GROUP, local_kv, query_group_width), masked_score, jnp.float32
        )
        running_sum = jnp.zeros((POSITION_GROUP, local_kv, query_group_width), jnp.float32)
        running_output = jnp.zeros(
            (POSITION_GROUP, local_kv, query_group_width, HEAD_WIDTH), jnp.float32
        )
        running_maximum, running_sum, running_output = lax.fori_loop(
            first_tile, last_tile + 1, add_tile, (running_maximum, running_sum, running_output)
        )
        return (running_output / running_sum[..., None]).astype(jnp.bfloat16)

    outputs = lax.map(one_tile, jnp.arange(row_count // POSITION_GROUP, dtype=jnp.int32))
    attn = outputs.reshape(row_count, local_q * HEAD_WIDTH)
    return lax.all_to_all(attn, "uly", split_axis=0, concat_axis=1, tiled=True)


def solution(mesh):
    placed = (P(("blk", "uly"), None), P(("blk", "uly"), None), P(("blk", "uly"), None), P("blk"))
    return jax.shard_map(
        local, mesh=mesh, in_specs=placed, out_specs=P(("blk", "uly"), None), check_vma=False
    )
```

profile of v0, /device:TPU:17, one launch (start us, length us, event | category | flops | bytes accessed | tf_op | source)
XLA Modules:
  0.0 92.5 jit_solution(1253593889368224903)
XLA Ops:
  0.0 1.7 %copy.24 = bf16[128,512]{0,1:T(8,128)(2,1)} copy(bf16[128,512]{1,0:T(8,128)(2,1)} %param.8) | data formatting | bytes 262144 | tf_op args[2]
  1.7 4.0 %all-to-all-start.2 = ((bf16[128,4,128]{0,2,1:T(8,128)(2,1)}), bf16[128,4,128]{0,2,1:T(8,128)(2,1)S(1)}, u32[]{:S(2)}, u32[]{:S(2)}) async-start(bf16[128,4,128]{0,2,1:T(8,128)(2,1)} %bitcast.5), calls=%async_computation.2 | async-start | bytes 262144 | tf_op jit(solution)/shard_map/all_to_all | solution.py:34
  5.7 0.7 copy_bitcast_fusion.1
  6.3 2.9 %all-to-all-done.2 = bf16[128,4,128]{0,2,1:T(8,128)(2,1)S(1)} async-done(((bf16[128,4,128]{0,2,1:T(8,128)(2,1)}), bf16[128,4,128]{0,2,1:T(8,128)(2,1)S(1)}, u32[]{:S(2)}, u32[]{:S(2)}) %all-to-all-start.2) | async-done | bytes 131104 | tf_op jit(solution)/shard_map/all_to_all | solution.py:34
  9.2 4.3 %all-to-all-start = ((bf16[128,4,128]{2,0,1:T(8,128)(2,1)}), bf16[128,4,128]{2,0,1:T(8,128)(2,1)S(1)}, u32[]{:S(2)}, u32[]{:S(2)}) async-start(bf16[128,4,128]{2,0,1:T(8,128)(2,1)} %copy_bitcast_fusion.1), calls=%async_computation | async-start | bytes 262144 | tf_op jit(solution)/shard_map/all_to_all | solution.py:33
  13.6 2.3 %copy.39 = bf16[16,4,8,1024]{3,2,0,1:T(8,128)(2,1)} copy(bf16[16,4,8,1024]{3,2,1,0:T(8,128)(2,1)} %bitcast.111) | data formatting | bytes 2097152 | tf_op jit(solution)/shard_map/all_to_all | solution.py:31
  15.9 1.3 %all-to-all-done = bf16[128,4,128]{2,0,1:T(8,128)(2,1)S(1)} async-done(((bf16[128,4,128]{2,0,1:T(8,128)(2,1)}), bf16[128,4,128]{2,0,1:T(8,128)(2,1)S(1)}, u32[]{:S(2)}, u32[]{:S(2)}) %all-to-all-start) | async-done | bytes 131104 | tf_op jit(solution)/shard_map/all_to_all | solution.py:33
  17.1 4.5 %all-to-all-start.1 = ((bf16[128,4,1024]{2,0,1:T(8,128)(2,1)}), bf16[128,4,1024]{2,0,1:T(8,128)(2,1)S(1)}, u32[]{:S(2)}, u32[]{:S(2)}) async-start(bf16[128,4,1024]{2,0,1:T(8,128)(2,1)} %bitcast.83), calls=%async_computation.1 | async-start | bytes 2097152 | tf_op jit(solution)/shard_map/all_to_all | solution.py:31
  21.7 0.1 copy.25
  21.8 3.2 %collective-permute-start.2 = (bf16[512,128]{1,0:T(8,128)(2,1)S(1)}, bf16[512,128]{1,0:T(8,128)(2,1)S(1)}, u32[]{:S(2)}, u32[]{:S(2)}) collective-permute-start(bf16[512,128]{1,0:T(8,128)(2,1)S(1)} %bitcast.116), channel_id=1, source_target_pairs={{0,8},{4,12},{8,16},{12,20},{16,24},{20,28},{1,9},{5,13},{9,17},{1... | collective-permute-start | bytes 393224 | tf_op jit(solution)/shard_map/ppermute | solution.py:17
  25.0 3.1 %collective-permute-start.3 = (bf16[512,128]{1,0:T(8,128)(2,1)S(1)}, bf16[512,128]{1,0:T(8,128)(2,1)S(1)}, u32[]{:S(2)}, u32[]{:S(2)}) collective-permute-start(bf16[512,128]{1,0:T(8,128)(2,1)S(1)} %bitcast.117), channel_id=1, source_target_pairs={{0,4},{4,8},{8,12},{12,16},{16,20},{20,24},{24,28},{1,5},{5,9},{9,... | collective-permute-start | bytes 393224 | tf_op jit(solution)/shard_map/ppermute | solution.py:17
  28.1 1.4 %reduce_min.10 = s32[]{:T(128)} reduce(s32[512]{0:T(512)} %param.9, s32[]{:T(128)} %constant.93.clone.1), dimensions={0}, to_apply=%region_0.1 | reduce | flops 511 | bytes 2056 | tf_op jit(solution)/shard_map/while/body/eval_jaxpr/reduce_min | solution.py:62
  30.2 1.9 %collective-permute-start = (bf16[512,128]{1,0:T(8,128)(2,1)S(1)}, bf16[512,128]{1,0:T(8,128)(2,1)S(1)}, u32[]{:S(2)}, u32[]{:S(2)}) collective-permute-start(bf16[512,128]{1,0:T(8,128)(2,1)S(1)} %bitcast.113), channel_id=1, source_target_pairs={{0,8},{4,12},{8,16},{12,20},{16,24},{20,28},{1,9},{5,13},{9,17},{1... | collective-permute-start | bytes 393224 | tf_op jit(solution)/shard_map/ppermute | solution.py:17
  32.2 1.9 %collective-permute-start.1 = (bf16[512,128]{1,0:T(8,128)(2,1)S(1)}, bf16[512,128]{1,0:T(8,128)(2,1)S(1)}, u32[]{:S(2)}, u32[]{:S(2)}) collective-permute-start(bf16[512,128]{1,0:T(8,128)(2,1)S(1)} %bitcast.114), channel_id=1, source_target_pairs={{0,4},{4,8},{8,12},{12,16},{16,20},{20,24},{24,28},{1,5},{5,9},{9,... | collective-permute-start | bytes 393224 | tf_op jit(solution)/shard_map/ppermute | solution.py:17
  34.1 0.8 maximum_bitcast_fusion.1
  34.9 1.7 %collective-permute-done = bf16[512,128]{1,0:T(8,128)(2,1)S(1)} collective-permute-done((bf16[512,128]{1,0:T(8,128)(2,1)S(1)}, bf16[512,128]{1,0:T(8,128)(2,1)S(1)}, u32[]{:S(2)}, u32[]{:S(2)}) %collective-permute-start) | collective-permute-done | bytes 131104 | tf_op jit(solution)/shard_map/ppermute | solution.py:17
  36.6 2.8 %collective-permute-done.1 = bf16[512,128]{1,0:T(8,128)(2,1)S(1)} collective-permute-done((bf16[512,128]{1,0:T(8,128)(2,1)S(1)}, bf16[512,128]{1,0:T(8,128)(2,1)S(1)}, u32[]{:S(2)}, u32[]{:S(2)}) %collective-permute-start.1) | collective-permute-done | bytes 131104 | tf_op jit(solution)/shard_map/ppermute | solution.py:17
  39.4 0.8 maximum_bitcast_fusion
  40.2 0.3 copy.36
  40.5 0.1 copy.26
  40.6 0.2 broadcast.67
  40.9 0.6 broadcast.66
  41.5 29.5 %while.24 = (s32[]{:T(128)}, f32[512,1,8]{0,2,1:T(8,128)S(1)}, f32[512,1,8]{0,2,1:T(8,128)}, f32[512,1,8,128]{0,3,2,1:T(8,128)S(1)}, s32[]{:T(128)}, /*index=5*/...) while((s32[]{:T(128)}, f32[512,1,8]{0,2,1:T(8,128)S(1)}, ...), condition=%wide.region_4.5_spmd.clone, body=%wide.region_1.4_spmd.clone.sunk | while | flops 1102853120 | bytes 32123144 | solution.py:102
  41.5 0.9 %compare_and_fusion.2 = pred[512,512]{0,1:T(8,128)(4,1)S(1)} fusion(s32[512]{0:T(512)S(1)} %get-tuple-element.256, s32[512]{0:T(512)} %get-tuple-element.295, s32[512]{0:T(512)S(1)} %get-tuple-element.257), kind=kLoop, calls=%fused_computation.12.clone.1 | loop fusion | flops 786432 | bytes 268288 | tf_op jit(solution)/shard_map/while/body/eval_jaxpr/while/body/and | solution.py:71
  42.5 2.4 %fusion.31 = (f32[512,8]{0,1:T(8,128)S(1)}, f32[512,512,8]{1,0,2:T(8,128)S(1)}) fusion(pred[512,512]{0,1:T(8,128)(4,1)S(1)} %compare_and_fusion.2, bf16[512,1,8,128]{3,0,2,1:T(8,128)(2,1)S(1)} %get-tuple-element.297, bf16[1536,1,128]{2,0,1:T(8,128)(2,1)} %get-tuple-element.296, s32[]{:T(128)S(6)} %select_n.64), kind=kOutput, calls=%fused_computation.3.clone.1 | convolution fusion | flops 543158272 | bytes 9846788 | tf_op jit(solution)/shard_map/while/body/eval_jaxpr/while/body/tkgd,nkd->tkgn/dot_general | solution.py:76
  44.9 0.0 copy-start.1
  44.9 3.7 %bitcast_add_fusion.5 = f32[512,1,8,128]{0,3,2,1:T(8,128)S(1)} fusion(f32[512,1,8,128]{0,3,2,1:T(8,128)S(1)} %get-tuple-element.279, f32[512,512,8]{1,0,2:T(8,128)S(1)} %get-tuple-element.260, f32[512,8]{0,1:T(8,128)S(1)} %bitcast.106, pred[512,512]{0,1:T(8,128)(4,1)S(1)} %compare_and_fusion.2, f32[512,8]{0,1:T(8,128)S(1)} %get-tuple-element.261, ...), kind=kOutput, calls=%fused_computation.9.clone.1 | convolution fusion | flops 548405248 | bytes 13008900 | tf_op jit(solution)/shard_map/while/body/eval_jaxpr/while/body/tkgn,nkd->tkgd/dot_general | solution.py:86
  48.6 2.0 %fusion.33 = f32[512,8]{0,1:T(8,128)S(1)} fusion(f32[512,512,8]{1,0,2:T(8,128)S(1)} %get-tuple-element.260, f32[512,8]{0,1:T(8,128)S(1)} %bitcast.107, pred[512,512]{0,1:T(8,128)(4,1)S(1)} %compare_and_fusion.2), kind=kLoop, calls=%fused_computation.5.clone.1 | loop fusion | flops 10481664 | bytes 8683520 | tf_op jit(solution)/shard_map/while/body/eval_jaxpr/while/body/reduce_sum | solution.py:85
  50.7 0.0 copy-start.2
  50.7 0.6 copy-done.2
  51.3 0.9 %compare_and_fusion.2 = pred[512,512]{0,1:T(8,128)(4,1)S(1)} fusion(s32[512]{0:T(512)S(1)} %get-tuple-element.256, s32[512]{0:T(512)} %get-tuple-element.295, s32[512]{0:T(512)S(1)} %get-tuple-element.257), kind=kLoop, calls=%fused_computation.12.clone.1 | loop fusion | flops 786432 | bytes 268288 | tf_op jit(solution)/shard_map/while/body/eval_jaxpr/while/body/and | solution.py:71
  52.3 2.4 %fusion.31 = (f32[512,8]{0,1:T(8,128)S(1)}, f32[512,512,8]{1,0,2:T(8,128)S(1)}) fusion(pred[512,512]{0,1:T(8,128)(4,1)S(1)} %compare_and_fusion.2, bf16[512,1,8,128]{3,0,2,1:T(8,128)(2,1)S(1)} %get-tuple-element.297, bf16[1536,1,128]{2,0,1:T(8,128)(2,1)} %get-tuple-element.296, s32[]{:T(128)S(6)} %select_n.64), kind=kOutput, calls=%fused_computation.3.clone.1 | convolution fusion | flops 543158272 | bytes 9846788 | tf_op jit(solution)/shard_map/while/body/eval_jaxpr/while/body/tkgd,nkd->tkgn/dot_general | solution.py:76
  54.7 0.0 copy-start.1
  54.7 3.7 %bitcast_add_fusion.5 = f32[512,1,8,128]{0,3,2,1:T(8,128)S(1)} fusion(f32[512,1,8,128]{0,3,2,1:T(8,128)S(1)} %get-tuple-element.279, f32[512,512,8]{1,0,2:T(8,128)S(1)} %get-tuple-element.260, f32[512,8]{0,1:T(8,128)S(1)} %bitcast.106, pred[512,512]{0,1:T(8,128)(4,1)S(1)} %compare_and_fusion.2, f32[512,8]{0,1:T(8,128)S(1)} %get-tuple-element.261, ...), kind=kOutput, calls=%fused_computation.9.clone.1 | convolution fusion | flops 548405248 | bytes 13008900 | tf_op jit(solution)/shard_map/while/body/eval_jaxpr/while/body/tkgn,nkd->tkgd/dot_general | solution.py:86
  58.5 2.0 %fusion.33 = f32[512,8]{0,1:T(8,128)S(1)} fusion(f32[512,512,8]{1,0,2:T(8,128)S(1)} %get-tuple-element.260, f32[512,8]{0,1:T(8,128)S(1)} %bitcast.107, pred[512,512]{0,1:T(8,128)(4,1)S(1)} %compare_and_fusion.2), kind=kLoop, calls=%fused_computation.5.clone.1 | loop fusion | flops 10481664 | bytes 8683520 | tf_op jit(solution)/shard_map/while/body/eval_jaxpr/while/body/reduce_sum | solution.py:85
  60.5 0.0 copy-start.2
  60.5 0.6 copy-done.2
  61.1 0.9 %compare_and_fusion.2 = pred[512,512]{0,1:T(8,128)(4,1)S(1)} fusion(s32[512]{0:T(512)S(1)} %get-tuple-element.256, s32[512]{0:T(512)} %get-tuple-element.295, s32[512]{0:T(512)S(1)} %get-tuple-element.257), kind=kLoop, calls=%fused_computation.12.clone.1 | loop fusion | flops 786432 | bytes 268288 | tf_op jit(solution)/shard_map/while/body/eval_jaxpr/while/body/and | solution.py:71
  62.1 2.4 %fusion.31 = (f32[512,8]{0,1:T(8,128)S(1)}, f32[512,512,8]{1,0,2:T(8,128)S(1)}) fusion(pred[512,512]{0,1:T(8,128)(4,1)S(1)} %compare_and_fusion.2, bf16[512,1,8,128]{3,0,2,1:T(8,128)(2,1)S(1)} %get-tuple-element.297, bf16[1536,1,128]{2,0,1:T(8,128)(2,1)} %get-tuple-element.296, s32[]{:T(128)S(6)} %select_n.64), kind=kOutput, calls=%fused_computation.3.clone.1 | convolution fusion | flops 543158272 | bytes 9846788 | tf_op jit(solution)/shard_map/while/body/eval_jaxpr/while/body/tkgd,nkd->tkgn/dot_general | solution.py:76
  64.5 3.7 %bitcast_add_fusion.5 = f32[512,1,8,128]{0,3,2,1:T(8,128)S(1)} fusion(f32[512,1,8,128]{0,3,2,1:T(8,128)S(1)} %get-tuple-element.279, f32[512,512,8]{1,0,2:T(8,128)S(1)} %get-tuple-element.260, f32[512,8]{0,1:T(8,128)S(1)} %bitcast.106, pred[512,512]{0,1:T(8,128)(4,1)S(1)} %compare_and_fusion.2, f32[512,8]{0,1:T(8,128)S(1)} %get-tuple-element.261, ...), kind=kOutput, calls=%fused_computation.9.clone.1 | convolution fusion | flops 548405248 | bytes 13008900 | tf_op jit(solution)/shard_map/while/body/eval_jaxpr/while/body/tkgn,nkd->tkgd/dot_general | solution.py:86
  68.3 2.0 %fusion.33 = f32[512,8]{0,1:T(8,128)S(1)} fusion(f32[512,512,8]{1,0,2:T(8,128)S(1)} %get-tuple-element.260, f32[512,8]{0,1:T(8,128)S(1)} %bitcast.107, pred[512,512]{0,1:T(8,128)(4,1)S(1)} %compare_and_fusion.2), kind=kLoop, calls=%fused_computation.5.clone.1 | loop fusion | flops 10481664 | bytes 8683520 | tf_op jit(solution)/shard_map/while/body/eval_jaxpr/while/body/reduce_sum | solution.py:85
  70.4 0.6 copy-done.2
  71.0 1.0 %divide_convert_fusion = bf16[512,1,8,128]{0,3,2,1:T(8,128)(2,1)S(1)} fusion(f32[512,1,8,128]{0,3,2,1:T(8,128)S(1)} %get-tuple-element.108, f32[512,8]{0,1:T(8,128)} %bitcast.112), kind=kLoop, calls=%fused_computation.28 | loop fusion | flops 1048576 | bytes 3162112 | tf_op jit(solution)/shard_map/while/body/eval_jaxpr/convert_element_type | solution.py:105
  72.0 0.3 reshape.124
  72.3 0.7 copy.32
  72.9 17.6 %all_to_all.73 = bf16[4,128,1024]{2,1,0:T(8,128)(2,1)S(1)} all-to-all(bf16[4,128,1024]{2,1,0:T(8,128)(2,1)S(1)} %copy.32), channel_id=1, replica_groups=mesh['blk'=8,'uly'=4] {'uly'}, dimensions={0} | all-to-all | bytes 2097152 | tf_op jit(solution)/shard_map/all_to_all | solution.py:109
  90.5 0.7 copy.29
  91.2 1.3 %copy.30 = bf16[128,4096]{1,0:T(8,128)(2,1)} copy(bf16[128,4096]{0,1:T(8,128)(2,1)S(1)} %bitcast.110) | data formatting | bytes 2097152 | tf_op jit(solution)/shard_map/all_to_all | solution.py:109
  (23 shorter events, 0.1 us)
Async XLA Ops:
  0.0 5.7 %copy-start = (bf16[128,512]{1,0:T(8,128)(2,1)S(1)}, bf16[128,512]{1,0:T(8,128)(2,1)}, u32[]{:S(2)}) copy-start(bf16[128,512]{1,0:T(8,128)(2,1)} %param.7) | copy-start | bytes 393220
  1.7 7.5 %all-to-all-start.2 = ((bf16[128,4,128]{0,2,1:T(8,128)(2,1)}), bf16[128,4,128]{0,2,1:T(8,128)(2,1)S(1)}, u32[]{:S(2)}, u32[]{:S(2)}) async-start(bf16[128,4,128]{0,2,1:T(8,128)(2,1)} %bitcast.5), calls=%async_computation.2 | async-start | bytes 262144 | tf_op jit(solution)/shard_map/all_to_all | solution.py:34
  9.2 7.9 %all-to-all-start = ((bf16[128,4,128]{2,0,1:T(8,128)(2,1)}), bf16[128,4,128]{2,0,1:T(8,128)(2,1)S(1)}, u32[]{:S(2)}, u32[]{:S(2)}) async-start(bf16[128,4,128]{2,0,1:T(8,128)(2,1)} %copy_bitcast_fusion.1), calls=%async_computation | async-start | bytes 262144 | tf_op jit(solution)/shard_map/all_to_all | solution.py:33
  17.1 23.0 %all-to-all-start.1 = ((bf16[128,4,1024]{2,0,1:T(8,128)(2,1)}), bf16[128,4,1024]{2,0,1:T(8,128)(2,1)S(1)}, u32[]{:S(2)}, u32[]{:S(2)}) async-start(bf16[128,4,1024]{2,0,1:T(8,128)(2,1)} %bitcast.83), calls=%async_computation.1 | async-start | bytes 2097152 | tf_op jit(solution)/shard_map/all_to_all | solution.py:31
  21.8 12.3 %collective-permute-start.2 = (bf16[512,128]{1,0:T(8,128)(2,1)S(1)}, bf16[512,128]{1,0:T(8,128)(2,1)S(1)}, u32[]{:S(2)}, u32[]{:S(2)}) collective-permute-start(bf16[512,128]{1,0:T(8,128)(2,1)S(1)} %bitcast.116), channel_id=1, source_target_pairs={{0,8},{4,12},{8,16},{12,20},{16,24},{20,28},{1,9},{5,13},{9,17},{1... | collective-permute-start | bytes 393224 | tf_op jit(solution)/shard_map/ppermute | solution.py:17
  25.0 9.1 %collective-permute-start.3 = (bf16[512,128]{1,0:T(8,128)(2,1)S(1)}, bf16[512,128]{1,0:T(8,128)(2,1)S(1)}, u32[]{:S(2)}, u32[]{:S(2)}) collective-permute-start(bf16[512,128]{1,0:T(8,128)(2,1)S(1)} %bitcast.117), channel_id=1, source_target_pairs={{0,4},{4,8},{8,12},{12,16},{16,20},{20,24},{24,28},{1,5},{5,9},{9,... | collective-permute-start | bytes 393224 | tf_op jit(solution)/shard_map/ppermute | solution.py:17
  30.2 6.3 %collective-permute-start = (bf16[512,128]{1,0:T(8,128)(2,1)S(1)}, bf16[512,128]{1,0:T(8,128)(2,1)S(1)}, u32[]{:S(2)}, u32[]{:S(2)}) collective-permute-start(bf16[512,128]{1,0:T(8,128)(2,1)S(1)} %bitcast.113), channel_id=1, source_target_pairs={{0,8},{4,12},{8,16},{12,20},{16,24},{20,28},{1,9},{5,13},{9,17},{1... | collective-permute-start | bytes 393224 | tf_op jit(solution)/shard_map/ppermute | solution.py:17
  32.2 7.2 %collective-permute-start.1 = (bf16[512,128]{1,0:T(8,128)(2,1)S(1)}, bf16[512,128]{1,0:T(8,128)(2,1)S(1)}, u32[]{:S(2)}, u32[]{:S(2)}) collective-permute-start(bf16[512,128]{1,0:T(8,128)(2,1)S(1)} %bitcast.114), channel_id=1, source_target_pairs={{0,4},{4,8},{8,12},{12,16},{16,20},{20,24},{24,28},{1,5},{5,9},{9,... | collective-permute-start | bytes 393224 | tf_op jit(solution)/shard_map/ppermute | solution.py:17
  44.9 5.8 %copy-start.1 = (f32[512,1,8]{0,2,1:T(8,128)S(1)}, f32[512,1,8]{0,2,1:T(8,128)}, u32[]{:S(2)}) copy-start(f32[512,1,8]{0,2,1:T(8,128)} %get-tuple-element.278) | copy-start | bytes 49156 | tf_op jit(solution)/shard_map/while/body/eval_jaxpr/while
  50.7 0.6 copy-start.2
  54.7 5.8 %copy-start.1 = (f32[512,1,8]{0,2,1:T(8,128)S(1)}, f32[512,1,8]{0,2,1:T(8,128)}, u32[]{:S(2)}) copy-start(f32[512,1,8]{0,2,1:T(8,128)} %get-tuple-element.278) | copy-start | bytes 49156 | tf_op jit(solution)/shard_map/while/body/eval_jaxpr/while
  60.5 0.6 copy-start.2
  64.5 5.8 %copy-start.1 = (f32[512,1,8]{0,2,1:T(8,128)S(1)}, f32[512,1,8]{0,2,1:T(8,128)}, u32[]{:S(2)}) copy-start(f32[512,1,8]{0,2,1:T(8,128)} %get-tuple-element.278) | copy-start | bytes 49156 | tf_op jit(solution)/shard_map/while/body/eval_jaxpr/while
  70.4 0.6 copy-start.2
where the time goes:
time: 92.6 us; the launch traced here: 92.5 us
  starting transfers between devices  23 us (25%)
  matrix products  18.4 us (20%)
  blocking collectives  17.6 us (19%)
  other arithmetic  13 us (14%)
  local copies, waits for them, and re-layouts  10.8 us (12%)
  waiting for transfers between devices  8.69 us (9%)
    all_to_all x1, blocking collectives, local(): return lax.all_to_all(attn, 'uly', split_axis=0, concat_axis=1, tiled=True)  17.6 us
    dot_general x3, matrix products, add_tile(): jnp.einsum('tkgn,nkd->tkgd', exps.astype(jnp.bfloat16), value_tile, prefe...  11.2 us
    ppermute x4, starting transfers between devices, from_behind(): return lax.ppermute(block, axis, route)  10.2 us
    dot_general x3, matrix products, add_tile(): jnp.einsum('tkgd,nkd->tkgn', query_tile, key_tile, preferred_element_type...  7.21 us
    reduce_sum x3, other arithmetic, add_tile(): running_sum = running_sum * factor + jnp.sum(exps, axis=-1)  6.1 us
    all_to_all x1, starting transfers between devices, local(): lax.all_to_all(query_projection, 'uly', split_axis=1, concat_axis=0, tile...  4.53 us
    ppermute x4, waiting for transfers between devices, from_behind(): return lax.ppermute(block, axis, route)  4.52 us
    all_to_all x1, starting transfers between devices, local(): lax.all_to_all(widen_heads(key_projection), 'uly', split_axis=1, concat_a...  4.33 us
  transfers between devices with their start and end apart: 7, of which 4 were waited for; matrix products, arithmetic and copies ran while one was open for 7% of the time, Pallas kernels for 0%

commit v1 on v0

v1 whole, which is shorter than its diff:
```python
import functools

import jax
import jax.numpy as jnp
from jax import lax
from jax.experimental import pallas as pl
from jax.experimental.pallas import tpu as pltpu
from jax.sharding import PartitionSpec as P

HEAD_WIDTH = 128
LOOK_BACK_BLOCKS = 2
MASKED = -1e30
LOG2_E = 1.4426950408889634
MESH = pl.DeviceIdType.MESH


def each(count, looped, body, first=0):
    if looped:
        pl.loop(first, count)(body)
    else:
        for index in range(first, count):
            body(index)


def when(condition):
    if isinstance(condition, bool):
        return lambda body: body() if condition else None
    return pl.when(condition)


def kernel(
    blocks, width, heads, group, batch,
    q_hbm, k_hbm, v_hbm, start_ref, o_hbm,
    q_ref, k_win, v_win, bias, o_ref,
    local_sem, out_sem, shift_sem, lane_sem, pair_sem, recv_sem,
):
    tokens = q_hbm.shape[0]
    keys = (2 * width + 1) * tokens
    pairs = width // 2
    looped = pairs > 2
    b, u = lax.axis_index("blk"), lax.axis_index("uly")
    g, c = u // 2, u % 2
    sibling = g * 2 + (1 - c)
    has_1, has_2 = b >= 1, b >= 2
    hbm, win = (k_hbm, v_hbm), (k_win, v_win)

    def slot(which, h, index):
        start = pl.multiple_of(index * tokens, tokens)
        return win[which].at[h, pl.ds(start, tokens), :]

    def own(which, h):
        return hbm[which].at[:, lanes(h)]

    def lanes(index, count=1):
        span = count * HEAD_WIDTH
        return pl.ds(pl.multiple_of(index * span, span), span)

    def remote(src, h, which, index, send, device):
        return pltpu.make_async_remote_copy(
            src_ref=src,
            dst_ref=slot(which, h, index),
            send_sem=send,
            recv_sem=recv_sem.at[h, which, index],
            device_id=device,
            device_id_type=MESH,
        )

    def arrived(h, index):
        for which in range(2):
            ref = slot(which, h, index)
            remote(ref, h, which, index, shift_sem.at[h, which, 0], (b, sibling)).wait_recv()

    def shift_copies(h, act):
        for distance in range(1, LOOK_BACK_BLOCKS + 1):
            @pl.when(b + distance < blocks)
            def _():
                for which in range(2):
                    act(remote(own(which, h), h, which, (distance - 1) * width + u,
                               shift_sem.at[h, which, distance - 1], (b + distance, u)))

    def lane_own(h, act):
        @functools.partial(each, pairs, looped, first=1)
        def _(j):
            other = (g + j) % pairs
            @pl.when(other > g)
            def _():
                for which in range(2):
                    act(remote(own(which, h), h, which, width + u,
                               lane_sem.at[h, which, j - 1, 0], (b, other * 2 + c)))

    def pair_own(h, act):
        @pl.when(c == 0)
        def _():
            for which in range(2):
                act(remote(own(which, h), h, which, width + u,
                           pair_sem.at[h, which, 0, 0], (b, sibling)))

    def relay_1(h, act):
        @pl.when(has_1)
        def _():
            @functools.partial(each, pairs, looped, first=1)
            def _(j):
                other = (g + j) % pairs
                for which in range(2):
                    act(remote(slot(which, h, u), h, which, u,
                               lane_sem.at[h, which, j - 1, 1], (b, other * 2 + c)))
            for which in range(2):
                act(remote(slot(which, h, u), h, which, u,
                           pair_sem.at[h, which, 0, 1], (b, sibling)))

    def relay_2(h, act):
        @pl.when(has_2)
        def _():
            @functools.partial(each, pairs, looped, first=1)
            def _(j):
                other = (g + j) % pairs
                @pl.when(other < g)
                def _():
                    for which in range(2):
                        act(remote(slot(which, h, width + u), h, which, width + u,
                                   lane_sem.at[h, which, j - 1, 0], (b, other * 2 + c)))
            @pl.when(c == 1)
            def _():
                for which in range(2):
                    act(remote(slot(which, h, width + u), h, which, width + u,
                               pair_sem.at[h, which, 0, 0], (b, sibling)))

    def forward(h, j, recent, act):
        other = (g + j) % pairs
        index = (0 if recent else width) + other * 2 + c
        for which in range(2):
            act(remote(slot(which, h, index), h, which, index,
                       pair_sem.at[h, which, j, 1 if recent else 0], (b, sibling)))

    def both(h, j, act, wait):
        other = (g + j) % pairs
        lane = other * 2 + c
        @pl.when(has_1)
        def _():
            if wait:
                arrived(h, lane)
            forward(h, j, True, act)
        @pl.when((other < g) | has_2)
        def _():
            if wait:
                arrived(h, width + lane)
            forward(h, j, False, act)

    def start(copy):
        copy.start()

    def sent(copy):
        copy.wait_send()

    def first_stage(h):
        @pl.when(has_1)
        def _():
            arrived(h, u)
        relay_1(h, start)
        @pl.when(has_2)
        def _():
            arrived(h, width + u)
        relay_2(h, start)

    def second_stage(h):
        each(pairs, looped, lambda j: both(h, j, start, True), first=1)

    def third_stage(h):
        @pl.when(has_1)
        def _():
            arrived(h, sibling)
        @pl.when((c == 1) | has_2)
        def _():
            arrived(h, width + sibling)
        @functools.partial(each, pairs, looped, first=1)
        def _(j):
            other = (g + j) % pairs
            @pl.when(has_1)
            def _():
                arrived(h, other * 2 + 1 - c)
            @pl.when((other < g) | has_2)
            def _():
                arrived(h, width + other * 2 + 1 - c)

    query_copy = pltpu.make_async_copy(q_hbm, q_ref, local_sem.at[0, 0, 1])
    query_copy.start()

    def own_copy(h, act):
        for which in range(2):
            act(pltpu.make_async_copy(
                own(which, h), slot(which, h, 2 * width), local_sem.at[h, which, 0]))

    each(heads, looped, lambda h: own_copy(h, start))

    @pl.when(b < LOOK_BACK_BLOCKS)
    def _():
        @functools.partial(each, heads, looped)
        def _(h):
            for ref in win:
                ref[h, 0 : 2 * width * tokens, :] = jnp.zeros(
                    (2 * width * tokens, HEAD_WIDTH), ref.dtype)

    barrier = pltpu.get_barrier_semaphore()
    for distance in range(1, LOOK_BACK_BLOCKS + 1):
        @pl.when(b + distance < blocks)
        def _():
            pl.semaphore_signal(barrier, inc=1, device_id=(b + distance, u), device_id_type=MESH)
        @pl.when(b - distance >= 0)
        def _():
            pl.semaphore_signal(barrier, inc=1, device_id=(b - distance, u), device_id_type=MESH)
    for j in range(1, pairs):
        pl.semaphore_signal(
            barrier, inc=1, device_id=(b, ((g + j) % pairs) * 2 + c), device_id_type=MESH)
    pl.semaphore_signal(barrier, inc=1, device_id=(b, sibling), device_id_type=MESH)
    after = jnp.minimum(blocks - 1 - b, LOOK_BACK_BLOCKS)
    pl.semaphore_wait(barrier, jnp.minimum(b, LOOK_BACK_BLOCKS) + after + pairs)

    each(heads, looped, lambda h: shift_copies(h, start))
    lane_own(0, start)
    pair_own(0, start)

    starts = jnp.broadcast_to(start_ref[pl.ds(u, 1), :], (tokens, tokens)).T
    row = lax.broadcasted_iota(jnp.int32, (tokens, tokens), 0)
    column = lax.broadcasted_iota(jnp.int32, (tokens, tokens), 1)
    place = (b * width + u) * tokens + row

    def mask_tile(index, piece):
        key_place = piece * tokens + column
        seen = (key_place >= starts) & (key_place <= place)
        bias[:, pl.ds(pl.multiple_of(index * tokens, tokens), tokens)] = jnp.where(
            seen, 0.0, MASKED)

    each(width, looped, lambda i: mask_tile(i, (b - 1) * width + i))
    each(width, looped,
         lambda i: mask_tile(width + i, jnp.where(i < u, b, b - 2) * width + i))
    mask_tile(2 * width, b * width + u)

    def out_copy(h):
        columns = lanes(h, group)
        return pltpu.make_async_copy(o_ref.at[:, columns], o_hbm.at[:, columns], out_sem.at[h])

    factor = HEAD_WIDTH ** (-0.5) * LOG2_E

    def attend(h, step):
        base = h * group + step * batch
        queries = jnp.concatenate(
            [q_ref[:, lanes(base + i)] for i in range(batch)],
            axis=0)
        scores = lax.dot_general(
            queries, k_win[h], (((1,), (1,)), ((), ())), preferred_element_type=jnp.float32)
        scores = scores.reshape(batch, tokens, keys) + bias[...][None]
        top = jnp.max(scores, axis=-1, keepdims=True)
        exps = jnp.exp2((scores - top) * factor)
        totals = jnp.sum(exps, axis=-1, keepdims=True)
        blended = jnp.dot(
            exps.astype(jnp.bfloat16).reshape(batch * tokens, keys), v_win[h],
            preferred_element_type=jnp.float32)
        result = (blended.reshape(batch, tokens, HEAD_WIDTH) / totals).astype(o_ref.dtype)
        for i in range(batch):
            o_ref[:, lanes(base + i)] = result[i]

    def head_sends(h):
        @when(h < heads)
        def _():
            first_stage(h)
        @when(h + 1 < heads)
        def _():
            lane_own(h + 1, start)
            pair_own(h + 1, start)

    head_sends(0)
    head_sends(1)
    second_stage(0)
    query_copy.wait()
    each(heads, looped, lambda h: own_copy(h, lambda copy: copy.wait()))
    steps = group // batch

    @functools.partial(each, heads, looped)
    def _(h):
        third_stage(h)
        head_sends(h + 2)
        each(steps // 2, looped, lambda step: attend(h, step))
        @when(h + 1 < heads)
        def _():
            second_stage(h + 1)
        each(steps, looped, lambda step: attend(h, step), first=steps // 2)
        out_copy(h).start()

    @functools.partial(each, heads, looped)
    def _(h):
        shift_copies(h, sent)
        lane_own(h, sent)
        pair_own(h, sent)
        relay_1(h, sent)
        relay_2(h, sent)
        each(pairs, looped, lambda j: both(h, j, sent, False), first=1)
        out_copy(h).wait()


def local(query_projection, key_projection, value_projection, doc_start):
    blocks, width = lax.axis_size("blk"), lax.axis_size("uly")
    tokens, query_columns = query_projection.shape
    heads = key_projection.shape[1] // HEAD_WIDTH
    group = query_columns // HEAD_WIDTH // heads
    keys = (2 * width + 1) * tokens
    batch = group
    while batch > 1 and batch * tokens * keys > 640 * 1024:
        batch //= 2
    pairs = width // 2
    hbm = pl.BlockSpec(memory_space=pl.ANY)
    return pl.pallas_call(
        functools.partial(kernel, blocks, width, heads, group, batch),
        out_shape=jax.ShapeDtypeStruct(query_projection.shape, query_projection.dtype),
        in_specs=[hbm, hbm, hbm, pl.BlockSpec(memory_space=pltpu.VMEM)],
        out_specs=hbm,
        scratch_shapes=[
            pltpu.VMEM((tokens, query_columns), jnp.bfloat16),
            pltpu.VMEM((heads, keys, HEAD_WIDTH), jnp.bfloat16),
            pltpu.VMEM((heads, keys, HEAD_WIDTH), jnp.bfloat16),
            pltpu.VMEM((tokens, keys), jnp.float32),
            pltpu.VMEM((tokens, query_columns), jnp.bfloat16),
            pltpu.SemaphoreType.DMA((heads, 2, 2)),
            pltpu.SemaphoreType.DMA((heads,)),
            pltpu.SemaphoreType.DMA((heads, 2, LOOK_BACK_BLOCKS)),
            pltpu.SemaphoreType.DMA((heads, 2, max(1, pairs - 1), 2)),
            pltpu.SemaphoreType.DMA((heads, 2, pairs, 2)),
            pltpu.SemaphoreType.DMA((heads, 2, 2 * width)),
        ],
        compiler_params=pltpu.CompilerParams(
            collective_id=0, has_side_effects=True, vmem_limit_bytes=60 * 1024 * 1024),
    )(query_projection, key_projection, value_projection, doc_start.reshape(width, tokens))


def solution(mesh):
    placed = (P(("blk", "uly"), None), P(("blk", "uly"), None), P(("blk", "uly"), None), P("blk"))
    return jax.shard_map(
        local, mesh=mesh, in_specs=placed, out_specs=P(("blk", "uly"), None), check_vma=False
    )
```

time: 92.6 us -> 30.8 us (0.33)
  Pallas kernels: 0 us -> 28.4 us
  starting transfers between devices: 23 us -> 0 us
  matrix products: 18.4 us -> 0 us
  blocking collectives: 17.6 us -> 0 us
  other arithmetic: 13 us -> 0 us
  waiting for transfers between devices: 8.69 us -> 0 us
  local copies, waits for them, and re-layouts: 10.8 us -> 2.29 us
    pallas_call x0 -> x1, Pallas kernels: none -> 28.4 us  [local(): pl.pallas_call(functools.partial(kernel, blocks, width, heads, group, bat...]
    dot_general x6 -> x0, matrix products: 18.4 us -> none  [the longest x3 11.2 us: add_tile(): jnp.einsum('tkgn,nkd->tkgd', exps.astype(jnp.bfloat16), value_tile, prefe...]
    all_to_all x1 -> x0, blocking collectives: 17.6 us -> none  [local(): return lax.all_to_all(attn, 'uly', split_axis=0, concat_axis=1, tiled=True)]
    all_to_all x3 -> x0, starting transfers between devices: 12.8 us -> none  [the longest x1 4.53 us: local(): lax.all_to_all(query_projection, 'uly', split_axis=1, concat_axis=0, tile...]
    ppermute x4 -> x0, starting transfers between devices: 10.2 us -> none  [from_behind(): return lax.ppermute(block, axis, route)]
    reduce_sum x3 -> x0, other arithmetic: 6.1 us -> none  [add_tile(): running_sum = running_sum * factor + jnp.sum(exps, axis=-1)]
    all_to_all x7 -> x0, local copies, waits for them, and re-layouts: 6.01 us -> none  [the longest x4 2.92 us: local(): return lax.all_to_all(attn, 'uly', split_axis=0, concat_axis=1, tiled=True)]
    ppermute x4 -> x0, waiting for transfers between devices: 4.52 us -> none  [from_behind(): return lax.ppermute(block, axis, route)]
  transfers between devices with their start and end apart: 7 -> 0, of which waited for: 4 -> 0; matrix products, arithmetic and copies ran while one was open for 7% -> 0% of each run, Pallas kernels for 0% -> 0%
where the time goes in v1:
time: 30.8 us; the launch traced here: 30.7 us
  Pallas kernels  28.4 us (92%)
  local copies, waits for them, and re-layouts  2.29 us (7%)
    pallas_call x1, Pallas kernels, local(): pl.pallas_call(functools.partial(kernel, blocks, width, heads, group, bat...  28.4 us
    unnamed x1, local copies, waits for them, and re-layouts  2.29 us

profile of v1, /device:TPU:17, one launch (start us, length us, event | category | flops | bytes accessed | tf_op | source)
XLA Modules:
  0.0 30.7 jit_solution(13513423404033575938)
XLA Ops:
  0.0 28.4 %shard_map.46 = bf16[128,4096]{1,0:T(8,128)(2,1)} custom-call(bf16[128,4096]{1,0:T(8,128)(2,1)} %q_hbm.1, bf16[128,512]{1,0:T(8,128)(2,1)} %k_hbm.1, bf16[128,512]{1,0:T(8,128)(2,1)} %v_hbm.1, s32[4,128]{1,0:T(4,128)} %bitcast.1), custom_call_target="tpu_custom_call" | custom-call | tf_op jit(solution)/shard_map/pallas_call | solution.py:311
  28.4 2.3 %copy.6 = bf16[128,4096]{1,0:T(8,128)(2,1)} copy(bf16[128,4096]{1,0:T(8,128)(2,1)} %shard_map.46) | data formatting | bytes 2097152

commit v2 on v1

v2 whole, which is shorter than its diff:
```python
import functools

import jax
import jax.numpy as jnp
from jax import lax
from jax.experimental import pallas as pl
from jax.experimental.pallas import tpu as pltpu
from jax.sharding import PartitionSpec as P

HEAD_WIDTH = 128
LOOK_BACK_BLOCKS = 2
MASKED = -1e30
LOG2_E = 1.4426950408889634
MESH = pl.DeviceIdType.MESH


def each(count, looped, body, first=0):
    if looped:
        pl.loop(first, count)(body)
    else:
        for index in range(first, count):
            body(index)


def when(condition):
    if isinstance(condition, bool):
        return lambda body: body() if condition else None
    return pl.when(condition)


def kernel(
    blocks, width, heads, group, batch,
    q_hbm, k_hbm, v_hbm, start_ref, o_ref,
    q_ref, k_near, v_near, k_far, v_far, near_bias, far_bias, top_ref, sum_ref,
    query_sem, local_sem, shift_sem, lane_sem, pair_sem, near_sem, far_sem,
):
    tokens = q_hbm.shape[0]
    pairs = width // 2
    others = width - 1
    looped = pairs > 2
    b, u = lax.axis_index("blk"), lax.axis_index("uly")
    g, c = u // 2, u % 2
    sibling = g * 2 + (1 - c)
    has_1, has_2 = b >= 1, b >= 2
    hbm, nears, fars = (k_hbm, v_hbm), (k_near, v_near), (k_far, v_far)

    def rows(index):
        return pl.ds(pl.multiple_of(index * tokens, tokens), tokens)

    def lanes(index, count=1):
        span = count * HEAD_WIDTH
        return pl.ds(pl.multiple_of(index * span, span), span)

    def near(which, h, distance):
        return nears[which].at[h, rows(LOOK_BACK_BLOCKS - distance), :]

    def far_index(part, lane, owner):
        return part * others + (lane - owner + width) % width - 1

    def own(which, h):
        return hbm[which].at[:, lanes(h)]

    def shift(h, which, distance, device):
        return pltpu.make_async_remote_copy(
            src_ref=own(which, h),
            dst_ref=near(which, h, distance),
            send_sem=shift_sem.at[h, which, distance - 1],
            recv_sem=near_sem.at[h, which, distance - 1],
            device_id=device,
            device_id_type=MESH,
        )

    def remote(src, h, which, part, lane, send, target):
        index = far_index(part, lane, target)
        return pltpu.make_async_remote_copy(
            src_ref=src,
            dst_ref=fars[which].at[h, rows(index), :],
            send_sem=send,
            recv_sem=far_sem.at[h, which, index],
            device_id=(b, target),
            device_id_type=MESH,
        )

    def near_arrived(h, distance):
        for which in range(2):
            shift(h, which, distance, (b, sibling)).wait_recv()

    def far_ref(which, h, part, lane):
        return fars[which].at[h, rows(far_index(part, lane, u)), :]

    def far_arrived(h, part, lane):
        index = far_index(part, lane, u)
        for which in range(2):
            ref = far_ref(which, h, part, lane)
            pltpu.make_async_remote_copy(
                src_ref=ref,
                dst_ref=ref,
                send_sem=pair_sem.at[h, which, 0, 0],
                recv_sem=far_sem.at[h, which, index],
                device_id=(b, sibling),
                device_id_type=MESH,
            ).wait_recv()

    def shift_copies(h, act):
        for distance in range(1, LOOK_BACK_BLOCKS + 1):
            @pl.when(b + distance < blocks)
            def _():
                for which in range(2):
                    act(shift(h, which, distance, (b + distance, u)))

    def own_copies(h, act):
        @functools.partial(each, pairs, looped, first=1)
        def _(j):
            other = (g + j) % pairs
            @pl.when(other > g)
            def _():
                for which in range(2):
                    act(remote(own(which, h), h, which, 1, u,
                               lane_sem.at[h, which, j - 1, 0], other * 2 + c))
        @pl.when(c == 0)
        def _():
            for which in range(2):
                act(remote(own(which, h), h, which, 1, u, pair_sem.at[h, which, 0, 0], sibling))

    def relay_1(h, act):
        @pl.when(has_1)
        def _():
            @functools.partial(each, pairs, looped, first=1)
            def _(j):
                other = (g + j) % pairs
                for which in range(2):
                    act(remote(near(which, h, 1), h, which, 0, u,
                               lane_sem.at[h, which, j - 1, 1], other * 2 + c))
            for which in range(2):
                act(remote(near(which, h, 1), h, which, 0, u,
                           pair_sem.at[h, which, 0, 1], sibling))

    def relay_2(h, act):
        @pl.when(has_2)
        def _():
            @functools.partial(each, pairs, looped, first=1)
            def _(j):
                other = (g + j) % pairs
                @pl.when(other < g)
                def _():
                    for which in range(2):
                        act(remote(near(which, h, 2), h, which, 1, u,
                                   lane_sem.at[h, which, j - 1, 0], other * 2 + c))
            @pl.when(c == 1)
            def _():
                for which in range(2):
                    act(remote(near(which, h, 2), h, which, 1, u,
                               pair_sem.at[h, which, 0, 0], sibling))

    def forward(h, j, act, wait):
        other = (g + j) % pairs
        lane = other * 2 + c
        for part, there in ((1, (other < g) | has_2), (0, has_1)):
            @pl.when(there)
            def _():
                if wait:
                    far_arrived(h, part, lane)
                for which in range(2):
                    act(remote(far_ref(which, h, part, lane), h, which, part, lane,
                               pair_sem.at[h, which, j, 1 - part], sibling))

    def start(copy):
        copy.start()

    def sent(copy):
        copy.wait_send()

    def first_stage(h):
        @pl.when(has_1)
        def _():
            near_arrived(h, 1)
        relay_1(h, start)
        @pl.when(has_2)
        def _():
            near_arrived(h, 2)
        relay_2(h, start)

    def second_stage(h):
        each(pairs, looped, lambda j: forward(h, j, start, True), first=1)

    def third_stage(h):
        @pl.when(has_1)
        def _():
            far_arrived(h, 0, sibling)
        @pl.when((c == 1) | has_2)
        def _():
            far_arrived(h, 1, sibling)
        @functools.partial(each, pairs, looped, first=1)
        def _(j):
            other = (g + j) % pairs
            @pl.when(has_1)
            def _():
                far_arrived(h, 0, other * 2 + 1 - c)
            @pl.when((other < g) | has_2)
            def _():
                far_arrived(h, 1, other * 2 + 1 - c)

    @pl.when(b < LOOK_BACK_BLOCKS)
    def _():
        @functools.partial(each, heads, looped)
        def _(h):
            for ref in nears:
                size = LOOK_BACK_BLOCKS * tokens
                ref[h, 0:size, :] = jnp.zeros((size, HEAD_WIDTH), ref.dtype)
            for ref in fars:
                ref[h] = jnp.zeros(ref.shape[1:], ref.dtype)

    barrier = pltpu.get_barrier_semaphore()
    for distance in range(1, LOOK_BACK_BLOCKS + 1):
        @pl.when(b + distance < blocks)
        def _():
            pl.semaphore_signal(barrier, inc=1, device_id=(b + distance, u), device_id_type=MESH)
        @pl.when(b - distance >= 0)
        def _():
            pl.semaphore_signal(barrier, inc=1, device_id=(b - distance, u), device_id_type=MESH)
    for j in range(1, pairs):
        pl.semaphore_signal(
            barrier, inc=1, device_id=(b, ((g + j) % pairs) * 2 + c), device_id_type=MESH)
    pl.semaphore_signal(barrier, inc=1, device_id=(b, sibling), device_id_type=MESH)

    query_copy = pltpu.make_async_copy(q_hbm, q_ref, query_sem)
    query_copy.start()

    def fetch(h, act):
        for which in range(2):
            act(pltpu.make_async_copy(own(which, h), near(which, h, 0), local_sem.at[h, which]))

    each(heads, looped, lambda h: fetch(h, start))

    after = jnp.minimum(blocks - 1 - b, LOOK_BACK_BLOCKS)
    pl.semaphore_wait(barrier, jnp.minimum(b, LOOK_BACK_BLOCKS) + after + pairs)

    shift_copies(0, start)
    own_copies(0, start)
    each(heads, looped, lambda h: shift_copies(h, start), first=1)

    starts = jnp.broadcast_to(start_ref[pl.ds(u, 1), :], (tokens, tokens)).T
    row = lax.broadcasted_iota(jnp.int32, (tokens, tokens), 0)
    column = lax.broadcasted_iota(jnp.int32, (tokens, tokens), 1)
    place = (b * width + u) * tokens + row

    def mask_tile(ref, index, piece):
        key_place = piece * tokens + column
        seen = (key_place >= starts) & (key_place <= place)
        ref[:, rows(index)] = jnp.where(seen, 0.0, MASKED)

    for distance in range(LOOK_BACK_BLOCKS + 1):
        mask_tile(near_bias, LOOK_BACK_BLOCKS - distance, (b - distance) * width + u)

    @functools.partial(each, others, looped)
    def _(i):
        lane = (u + 1 + i) % width
        mask_tile(far_bias, i, (b - 1) * width + lane)
        mask_tile(far_bias, others + i, jnp.where(lane < u, b, b - 2) * width + lane)

    factor = HEAD_WIDTH ** (-0.5) * LOG2_E

    def scores_of(h, first, count, k_ref, bias):
        queries = jnp.concatenate(
            [q_ref[:, lanes(h * group + first + i)] for i in range(count)], axis=0)
        scores = lax.dot_general(
            queries, k_ref[h], (((1,), (1,)), ((), ())), preferred_element_type=jnp.float32)
        scores = scores.reshape(count, tokens, bias.shape[1]) + bias[...][None]
        scores = scores.reshape(count * tokens, bias.shape[1])
        return scores, jnp.max(scores, axis=-1, keepdims=True)

    def blend(scores, top, v_ref, h):
        weights = jnp.exp2((scores - top) * factor).astype(jnp.bfloat16)
        ones = jnp.ones((v_ref.shape[1], HEAD_WIDTH), jnp.bfloat16)
        values = jnp.concatenate([v_ref[h], ones], axis=1)
        return jnp.dot(weights, values, preferred_element_type=jnp.float32)

    def span(first, count):
        return pl.ds(pl.multiple_of(first * tokens, tokens), count * tokens)

    def attend_near(h):
        scores, top = scores_of(h, 0, group, k_near, near_bias)
        sum_ref[h] = blend(scores, top, v_near, h)
        top_ref[h] = jnp.broadcast_to(top, (group * tokens, HEAD_WIDTH))

    def attend_far(h, step):
        part = span(step * batch, batch)
        scores, top = scores_of(h, step * batch, batch, k_far, far_bias)
        before = top_ref[h, part, :]
        top = jnp.maximum(before[:, :1], top)
        fade = jnp.exp2((before - top) * factor)
        total = blend(scores, top, v_far, h)
        before = sum_ref[h, part, :]
        blended = before[:, :HEAD_WIDTH] * fade + total[:, :HEAD_WIDTH]
        totals = before[:, HEAD_WIDTH:] * fade + total[:, HEAD_WIDTH:]
        result = (blended / totals).astype(o_ref.dtype)
        for i in range(batch):
            o_ref[:, lanes(h * group + step * batch + i)] = result[i * tokens : (i + 1) * tokens]

    query_copy.wait()
    each(heads, looped, lambda h: fetch(h, lambda copy: copy.wait()))

    @functools.partial(each, heads, looped)
    def _(h):
        first_stage(h)
        @when(h + 1 < heads)
        def _():
            own_copies(h + 1, start)
        @when(h == heads - 1)
        def _():
            second_stage(0)
        attend_near(h)

    steps = group // batch

    @functools.partial(each, heads, looped)
    def _(h):
        third_stage(h)
        each(steps // 2, looped, lambda step: attend_far(h, step))
        @when(h + 1 < heads)
        def _():
            second_stage(h + 1)
        each(steps, looped, lambda step: attend_far(h, step), first=steps // 2)

    @functools.partial(each, heads, looped)
    def _(h):
        shift_copies(h, sent)
        own_copies(h, sent)
        relay_1(h, sent)
        relay_2(h, sent)
        each(pairs, looped, lambda j: forward(h, j, sent, False), first=1)


def local(query_projection, key_projection, value_projection, doc_start):
    blocks, width = lax.axis_size("blk"), lax.axis_size("uly")
    tokens, query_columns = query_projection.shape
    heads = key_projection.shape[1] // HEAD_WIDTH
    group = query_columns // HEAD_WIDTH // heads
    near_keys = (LOOK_BACK_BLOCKS + 1) * tokens
    far_keys = LOOK_BACK_BLOCKS * (width - 1) * tokens
    batch = group
    while batch > 1 and batch * tokens * far_keys > 640 * 1024:
        batch //= 2
    pairs = width // 2
    hbm = pl.BlockSpec(memory_space=pl.ANY)
    vmem = pl.BlockSpec(memory_space=pltpu.VMEM)
    return pl.pallas_call(
        functools.partial(kernel, blocks, width, heads, group, batch),
        out_shape=pltpu.VMEM(query_projection.shape, query_projection.dtype),
        in_specs=[hbm, hbm, hbm, vmem],
        out_specs=vmem,
        scratch_shapes=[
            pltpu.VMEM((tokens, query_columns), jnp.bfloat16),
            pltpu.VMEM((heads, near_keys, HEAD_WIDTH), jnp.bfloat16),
            pltpu.VMEM((heads, near_keys, HEAD_WIDTH), jnp.bfloat16),
            pltpu.VMEM((heads, far_keys, HEAD_WIDTH), jnp.bfloat16),
            pltpu.VMEM((heads, far_keys, HEAD_WIDTH), jnp.bfloat16),
            pltpu.VMEM((tokens, near_keys), jnp.float32),
            pltpu.VMEM((tokens, far_keys), jnp.float32),
            pltpu.VMEM((heads, group * tokens, HEAD_WIDTH), jnp.float32),
            pltpu.VMEM((heads, group * tokens, 2 * HEAD_WIDTH), jnp.float32),
            pltpu.SemaphoreType.DMA,
            pltpu.SemaphoreType.DMA((heads, 2)),
            pltpu.SemaphoreType.DMA((heads, 2, LOOK_BACK_BLOCKS)),
            pltpu.SemaphoreType.DMA((heads, 2, max(1, pairs - 1), 2)),
            pltpu.SemaphoreType.DMA((heads, 2, pairs, 2)),
            pltpu.SemaphoreType.DMA((heads, 2, LOOK_BACK_BLOCKS)),
            pltpu.SemaphoreType.DMA((heads, 2, 2 * (width - 1))),
        ],
        compiler_params=pltpu.CompilerParams(
            collective_id=0, has_side_effects=True, vmem_limit_bytes=56 * 1024 * 1024),
    )(query_projection, key_projection, value_projection, doc_start.reshape(width, tokens))


def solution(mesh):
    placed = (P(("blk", "uly"), None), P(("blk", "uly"), None), P(("blk", "uly"), None), P("blk"))
    return jax.shard_map(
        local, mesh=mesh, in_specs=placed, out_specs=P(("blk", "uly"), None), check_vma=False
    )
```

time: 30.8 us -> 30.1 us (0.977)
  local copies, waits for them, and re-layouts: 2.29 us -> 0.97 us
    unnamed x1, local copies, waits for them, and re-layouts: 2.29 us -> 0.97 us
    pallas_call x1, Pallas kernels: 28.4 us -> 28.7 us  [local(): pl.pallas_call(functools.partial(kernel, blocks, width, heads, group, bat...]
where the time goes in v2:
time: 30.1 us; the launch traced here: 29.7 us
  Pallas kernels  28.7 us (95%)
  local copies, waits for them, and re-layouts  0.97 us (3%)
    pallas_call x1, Pallas kernels, local(): pl.pallas_call(functools.partial(kernel, blocks, width, heads, group, bat...  28.7 us
    unnamed x1, local copies, waits for them, and re-layouts  0.97 us

profile of v2, /device:TPU:17, one launch (start us, length us, event | category | flops | bytes accessed | tf_op | source)
XLA Modules:
  0.0 29.7 jit_solution(11572282367072621922)
XLA Ops:
  0.0 28.7 %shard_map.46 = bf16[128,4096]{1,0:T(8,128)(2,1)S(1)} custom-call(bf16[128,4096]{1,0:T(8,128)(2,1)} %q_hbm.1, bf16[128,512]{1,0:T(8,128)(2,1)} %k_hbm.1, bf16[128,512]{1,0:T(8,128)(2,1)} %v_hbm.1, s32[4,128]{1,0:T(4,128)} %bitcast.1), custom_call_target="tpu_custom_call" | custom-call | tf_op jit(solution)/shard_map/pallas_call | solution.py:347
  28.7 1.0 %copy.6 = bf16[128,4096]{1,0:T(8,128)(2,1)} copy(bf16[128,4096]{1,0:T(8,128)(2,1)S(1)} %shard_map.46) | data formatting | bytes 2097152

commit v3 on v2

--- a/solution.py
+++ b/solution.py
@@ -300,27 +300,33 @@
     query_copy.wait()
     each(heads, looped, lambda h: fetch(h, lambda copy: copy.wait()))
 
-    @functools.partial(each, heads, looped)
-    def _(h):
-        first_stage(h)
+    def take(h):
+        @when(h < heads)
+        def _():
+            first_stage(h)
         @when(h + 1 < heads)
         def _():
             own_copies(h + 1, start)
-        @when(h == heads - 1)
-        def _():
-            second_stage(0)
-        attend_near(h)
-
+
+    take(0)
+    attend_near(0)
+    take(1)
+    second_stage(0)
+    attend_near(1)
     steps = group // batch
 
     @functools.partial(each, heads, looped)
     def _(h):
         third_stage(h)
         each(steps // 2, looped, lambda step: attend_far(h, step))
+        take(h + 2)
         @when(h + 1 < heads)
         def _():
             second_stage(h + 1)
         each(steps, looped, lambda step: attend_far(h, step), first=steps // 2)
+        @when(h + 2 < heads)
+        def _():
+            attend_near(h + 2)
 
     @functools.partial(each, heads, looped)
     def _(h):

time: 30.1 us -> 28.6 us (0.950)
  Pallas kernels: 28.7 us -> 27.5 us
    pallas_call x1, Pallas kernels: 28.7 us -> 27.5 us  [local(): pl.pallas_call(functools.partial(kernel, blocks, width, heads, group, bat...]
where the time goes in v3:
time: 28.6 us; the launch traced here: 28.4 us
  Pallas kernels  27.5 us (96%)
  local copies, waits for them, and re-layouts  0.97 us (3%)
    pallas_call x1, Pallas kernels, local(): pl.pallas_call(functools.partial(kernel, blocks, width, heads, group, bat...  27.5 us
    unnamed x1, local copies, waits for them, and re-layouts  0.97 us

profile of v3, /device:TPU:17, one launch (start us, length us, event | category | flops | bytes accessed | tf_op | source)
XLA Modules:
  0.0 28.4 jit_solution(18394002901914077033)
XLA Ops:
  0.0 27.5 %shard_map.46 = bf16[128,4096]{1,0:T(8,128)(2,1)S(1)} custom-call(bf16[128,4096]{1,0:T(8,128)(2,1)} %q_hbm.1, bf16[128,512]{1,0:T(8,128)(2,1)} %k_hbm.1, bf16[128,512]{1,0:T(8,128)(2,1)} %v_hbm.1, s32[4,128]{1,0:T(4,128)} %bitcast.1), custom_call_target="tpu_custom_call" | custom-call | tf_op jit(solution)/shard_map/pallas_call | solution.py:353
  27.5 1.0 %copy.6 = bf16[128,4096]{1,0:T(8,128)(2,1)} copy(bf16[128,4096]{1,0:T(8,128)(2,1)S(1)} %shard_map.46) | data formatting | bytes 2097152
